TPU v7x, 32 devices: a whole 2x2x4 slice. The times are simulated.
32 devices in a mesh: outer: 4 (over y, core), inner: 8 (over z, x).
Axes of the slice: x: 2, y: 2, z: 4, core: 2. Of those that a mesh axis runs over, the one named last changes fastest.
Arguments:
- queries: bfloat16 [4096, 2048], P(('outer', 'inner')), may hold values from -6 to 6
- keys: bfloat16 [4096, 2048], P(('outer', 'inner')), may hold values from -6 to 6
- values: bfloat16 [4096, 2048], P(('outer', 'inner')), may hold values from -6 to 6
- gain: float32 [2048], replicated, may hold values from 0.5 to 1.5
Outputs:
- attended: bfloat16 [4096, 2048], P(('outer', 'inner'))
All inputs are finite; a program needn't handle non-finite values.
Results may differ from a plain program's by a relative error of at most 0.0049.
Values sent between devices are 32-bit elements; how exact they have to be, the bound alone decides.
No kernel may reach another device: no remote copies, remote signals or barrier semaphores. Data moves between devices by JAX's collectives and lax.ppermute only.
A program may use at most 64 MiB of HBM per device.

v0:
```python
import jax
import jax.numpy as jnp
from jax import lax
from jax.sharding import PartitionSpec as P

HEADS = 16
HEAD_DIM = 128
STRETCH = 128


def entering(value, axis, join, neutral):
    count, mine = (lax.axis_size(axis), lax.axis_index(axis))
    pieces = lax.all_gather(value, axis)
    running = jnp.full_like(value, 0) + jnp.asarray(neutral, value.dtype)

    def turn(position, running):
        longer = join(running, pieces[position])
        return jnp.where(position < mine, longer, running)

    return lax.fori_loop(0, count - 1, turn, running)


def add_states(earlier, later):
    return earlier + later


def on_device(queries, keys, values, gain):
    tok_rows = queries.shape[0]
    nblocks = tok_rows // STRETCH
    q_blocks = queries.reshape(nblocks, STRETCH, HEADS, HEAD_DIM)
    k_blocks = keys.reshape(nblocks, STRETCH, HEADS, HEAD_DIM)
    v_blocks = values.reshape(nblocks, STRETCH, HEADS, HEAD_DIM)
    block_states = jnp.einsum(
        "ckhd,ckhe->chde", k_blocks, v_blocks, preferred_element_type=jnp.float32
    )
    own_state = jnp.sum(block_states, axis=0)
    zero_state = jnp.zeros_like(own_state)
    within = entering(own_state, "inner", add_states, zero_state)
    share = lax.psum_scatter(own_state, "inner", scatter_dimension=1, tiled=True)
    share_before = entering(share, "outer", add_states, jnp.zeros_like(share))
    before = lax.all_gather(share_before, "inner", axis=1, tiled=True)
    incoming = before + within
    local_before = jnp.concatenate(
        [jnp.zeros_like(block_states), jnp.cumsum(block_states[:-1], axis=0)], axis=0
    )
    carried_bf = (incoming[None] + local_before).astype(jnp.bfloat16)
    causal = jnp.arange(STRETCH)[:, None] >= jnp.arange(STRETCH)[None, :]
    scores = jnp.einsum("cqhd,ckhd->chqk", q_blocks, k_blocks, preferred_element_type=jnp.float32)
    scores = jnp.where(causal[None, None], scores, 0.0).astype(jnp.bfloat16)
    raw = jnp.einsum("chqk,ckhd->cqhd", scores, v_blocks, preferred_element_type=jnp.float32)
    raw = raw + jnp.einsum(
        "cqhd,chde->cqhe", q_blocks, carried_bf, preferred_element_type=jnp.float32
    )
    scale = lax.rsqrt(jnp.mean(raw * raw, axis=-1, keepdims=True) + 1e-06)
    normed = raw * scale * gain.reshape(HEADS, HEAD_DIM)[None, None]
    return normed.astype(jnp.bfloat16).reshape(tok_rows, HEADS * HEAD_DIM)


def solution(mesh):
    return jax.shard_map(
        on_device,
        mesh=mesh,
        in_specs=(
            P(("outer", "inner"), None),
            P(("outer", "inner"), None),
            P(("outer", "inner"), None),
            P(),
        ),
        out_specs=P(("outer", "inner"), None),
        check_vma=False,
    )
```

profile of v0, /device:TPU:0, one launch (start us, length us, event | category | flops | bytes accessed | tf_op | source)
XLA Modules:
  0.0 253.1 jit_solution(3675425433769225967)
XLA Ops:
  6.5 0.0 copy-start
  6.5 0.0 reduce-scatter.2.cloned.1.call-start
  6.5 1.4 copy.18
  7.9 2.3 fusion.3
  10.2 0.0 reduce-scatter.2.cloned.1.call-update
  10.2 0.0 all-gather.7.cloned.1.call-start
  10.3 0.7 all-gather.7.cloned.1.call-update
  11.0 0.0 all-gather.5.cloned.1.call-start
  11.1 0.0 copy-done
  11.1 1.7 convolution_bitcast_fusion
  12.8 65.4 %reduce-scatter.2.cloned.1.call-done = f32[16,16,128]{2,1,0:T(8,128)} async-done(((f32[16,128,128]{2,1,0:T(8,128)}), f32[16,16,128]{2,1,0:T(8,128)}) %reduce-scatter.2.cloned.1.call-update) | async-done | bytes 131088 | tf_op jit(solution)/shard_map/reduce_scatter | solution.py:39
  78.2 7.3 %all-gather = f32[64,16,128]{2,1,0:T(8,128)S(1)} all-gather(f32[16,16,128]{2,1,0:T(8,128)} %reduce-scatter.2.cloned.1.call-done), channel_id=2, replica_groups=mesh['outer'=4,'inner'=8] {'outer'}, dimensions={0}, use_global_device_ids=true | all-gather | bytes 655360 | tf_op jit(solution)/shard_map/all_gather | solution.py:13
  85.5 0.2 while.28
  85.7 0.0 copy-start.1
  85.7 0.6 copy-done.1
  86.4 0.0 all-gather.5.cloned.1.call-update
  86.4 117.4 %all-gather.7.cloned.1.call-done = f32[128,128,128]{2,1,0:T(8,128)} async-done(((f32[16,128,128]{2,1,0:T(8,128)}), f32[128,128,128]{2,1,0:T(8,128)}) %all-gather.7.cloned.1.call-update) | async-done | bytes 8388624 | tf_op jit(solution)/shard_map/all_gather | solution.py:13
  203.8 0.0 copy-start.2
  203.8 11.3 %while.29 = (s32[]{:T(128)}, f32[16,128,128]{2,1,0:T(8,128)S(1)}, s32[]{:T(128)}, f32[8,16,128,128]{3,2,1,0:T(8,128)}, s32[]{:T(128)}, /*index=5*/s32[]{:T(128)}) while((s32[]{:T(128)}, f32[16,128,128]{2,1,0:T(8,128)S(1)}, s32[]{:T(128)}, f32[8,16,128,128]{3,2,1,0:T(8,128)}, s32[]{:T(128)}, /*index=5*/s32[]{:T(128)}) %tuple.72), condition=%wide.region_4.5_spmd.clone, body=%wide.region_3.4_spmd.clone.sunk | while | flops 786436 | bytes 3145821 | solution.py:20
  203.8 1.6 add_select_fusion.5
  205.4 1.6 add_select_fusion.5
  207.0 1.6 add_select_fusion.5
  208.6 1.6 add_select_fusion.5
  210.3 1.6 add_select_fusion.5
  211.9 1.6 add_select_fusion.5
  213.5 1.6 add_select_fusion.5
  215.1 28.3 %all-gather.5.cloned.1.call-done = f32[16,128,128]{2,1,0:T(8,128)} async-done(((f32[16,16,128]{2,1,0:T(8,128)}), f32[16,128,128]{2,1,0:T(8,128)}) %all-gather.5.cloned.1.call-update) | async-done | bytes 1048592 | tf_op jit(solution)/shard_map/all_gather | solution.py:41
  243.4 1.7 multiply_reduce_fusion
  245.2 0.0 copy-done.2
  245.2 0.3 multiply_convert_fusion
  245.6 1.0 copy.16
  (7 shorter events, 0.1 us)
Async XLA Ops:
  6.5 4.6 %copy-start = (bf16[128,2048]{1,0:T(8,128)(2,1)S(1)}, bf16[128,2048]{1,0:T(8,128)(2,1)}, u32[]{:S(2)}) copy-start(bf16[128,2048]{1,0:T(8,128)(2,1)} %param.8) | copy-start | bytes 1572868
  6.5 71.7 %reduce-scatter.2.cloned.1.call-start = ((), (), s32[]{:S(2)}) async-start(), calls=%async_computation.1 | async-start | bytes 1179648 | tf_op jit(solution)/shard_map/reduce_scatter | solution.py:39
  10.2 193.5 %all-gather.7.cloned.1.call-start = ((), (), s32[]{:S(2)}) async-start(), calls=%async_computation.3 | async-start | bytes 9437184 | tf_op jit(solution)/shard_map/all_gather | solution.py:13
  11.0 232.5 %all-gather.5.cloned.1.call-start = ((), (), s32[]{:S(2)}) async-start(), calls=%async_computation.2 | async-start | bytes 1179648 | tf_op jit(solution)/shard_map/all_gather | solution.py:41
  85.7 0.7 copy-start.1
  203.8 41.4 %copy-start.2 = (f32[2048]{0:T(1024)S(1)}, f32[2048]{0:T(1024)}, u32[]{:S(2)}) copy-start(f32[2048]{0:T(1024)} %param.11) | copy-start | bytes 24580
Sparse Core Ops, SparseCore 0:
  10.7 67.4 reduce-scatter.1
  80.3 123.3 all-gather.6
  205.8 37.5 all-gather.4
where the time goes:
time: 254 us; the launch traced here: 253 us
  waiting for transfers between devices  212 us (83%)
  between operations  13.2 us (5%)
  other arithmetic  11.7 us (5%)
  blocking collectives  7.33 us (3%)
  matrix products  5.74 us (2%)
  local copies, waits for them, and re-layouts  3.03 us (1%)
    all_gather x1, waiting for transfers between devices, entering(): pieces = lax.all_gather(value, axis)  117 us
    reduce_scatter x1, waiting for transfers between devices, on_device(): lax.psum_scatter(own_state, 'inner', scatter_dimension=1, tiled=True)  65.4 us
    all_gather x1, waiting for transfers between devices, on_device(): before = lax.all_gather(share_before, 'inner', axis=1, tiled=True)  28.3 us
    select_n x10, other arithmetic, turn(): return jnp.where(position < mine, longer, running)  11.3 us
    all_gather x1, blocking collectives, entering(): pieces = lax.all_gather(value, axis)  7.33 us
  transfers between devices with their start and end apart: 3, of which 3 were waited for; matrix products, arithmetic and copies ran while one was open for 5% of the time, Pallas kernels for 0%

commit v1 on v0

--- a/solution.py
+++ b/solution.py
@@ -38,7 +38,14 @@
     within = entering(own_state, "inner", add_states, zero_state)
     share = lax.psum_scatter(own_state, "inner", scatter_dimension=1, tiled=True)
     share_before = entering(share, "outer", add_states, jnp.zeros_like(share))
-    before = lax.all_gather(share_before, "inner", axis=1, tiled=True)
+    size = lax.axis_size("inner")
+    hops = [(i, (i + 1) % size) for i in range(size)]
+    parts = [share_before]
+    for stride in range(1, size):
+        parts = [lax.ppermute(parts[0], "inner", hops), *parts]
+    out = jnp.concatenate(parts, axis=1)
+    shift = (lax.axis_index("inner") + 1) * parts[-1].shape[1]
+    before = jnp.roll(out, shift, axis=1)
     incoming = before + within
     local_before = jnp.concatenate(
         [jnp.zeros_like(block_states), jnp.cumsum(block_states[:-1], axis=0)], axis=0

time: 254 us -> 240 us (0.945)
  waiting for transfers between devices: 212 us -> 181 us
  local copies, waits for them, and re-layouts: 3.03 us -> 19.7 us
    all_gather x1, waiting for transfers between devices: 117 us -> 43.9 us  [entering(): pieces = lax.all_gather(value, axis)]
    ppermute x0 -> x7, waiting for transfers between devices: none -> 69.5 us  [on_device(): parts = [lax.ppermute(parts[0], 'inner', hops), *parts]]
    all_gather x1 -> x0, waiting for transfers between devices: 28.3 us -> none  [on_device(): before = lax.all_gather(share_before, 'inner', axis=1, tiled=True)]
    unnamed x6 -> x33, local copies, waits for them, and re-layouts: 0.66 us -> 16.6 us
  transfers between devices with their start and end apart: 3 -> 9, of which waited for: 3 -> 9; matrix products, arithmetic and copies ran while one was open for 5% -> 8% of each run, Pallas kernels for 0% -> 0%
where the time goes in v1:
time: 240 us
  waiting for transfers between devices  181 us (75%)
  local copies, waits for them, and re-layouts  19.7 us (8%)
  between operations  13.6 us (6%)
  other arithmetic  11.6 us (5%)
  blocking collectives  7.33 us (3%)
  matrix products  4.73 us (2%)
    ppermute x7, waiting for transfers between devices, on_device(): parts = [lax.ppermute(parts[0], 'inner', hops), *parts]  69.5 us
    reduce_scatter x1, waiting for transfers between devices, on_device(): lax.psum_scatter(own_state, 'inner', scatter_dimension=1, tiled=True)  67.2 us
    all_gather x1, waiting for transfers between devices, entering(): pieces = lax.all_gather(value, axis)  43.9 us
    unnamed x33, local copies, waits for them, and re-layouts  16.6 us
    select_n x10, other arithmetic, turn(): return jnp.where(position < mine, longer, running)  11.2 us
    all_gather x1, blocking collectives, entering(): pieces = lax.all_gather(value, axis)  7.33 us
  transfers between devices with their start and end apart: 9, of which 9 were waited for; matrix products, arithmetic and copies ran while one was open for 8% of the time, Pallas kernels for 0%

profile of v1, /device:TPU:0, one launch (start us, length us, event | category | flops | bytes accessed | tf_op | source)
XLA Modules:
  0.0 239.6 jit_solution(1578989103899441874)
XLA Ops:
  6.5 1.4 copy.18
  7.9 2.3 fusion.3
  11.0 67.2 %reduce-scatter.2.cloned.1.call-done = f32[16,16,128]{2,1,0:T(8,128)} async-done(((f32[16,128,128]{2,1,0:T(8,128)}), f32[16,16,128]{2,1,0:T(8,128)}) %reduce-scatter.2.cloned.1.call-update) | async-done | bytes 131088 | tf_op jit(solution)/shard_map/reduce_scatter | solution.py:39
  78.2 7.3 %all-gather = f32[64,16,128]{2,1,0:T(8,128)S(1)} all-gather(f32[16,16,128]{2,1,0:T(8,128)} %reduce-scatter.2.cloned.1.call-done), channel_id=2, replica_groups=mesh['outer'=4,'inner'=8] {'outer'}, dimensions={0}, use_global_device_ids=true | all-gather | bytes 655360 | tf_op jit(solution)/shard_map/all_gather | solution.py:13
  85.7 1.2 collective-permute-start
  86.9 8.5 %collective-permute-done = f32[16,16,128]{2,1,0:T(8,128)S(1)} collective-permute-done((f32[16,16,128]{2,1,0:T(8,128)S(1)}, f32[16,16,128]{2,1,0:T(8,128)S(1)}, u32[]{:S(2)}, u32[]{:S(2)}) %collective-permute-start) | collective-permute-done | bytes 131104 | tf_op jit(solution)/shard_map/ppermute | solution.py:45
  95.4 11.0 %collective-permute-done.1 = f32[16,16,128]{2,1,0:T(8,128)S(1)} collective-permute-done((f32[16,16,128]{2,1,0:T(8,128)S(1)}, f32[16,16,128]{2,1,0:T(8,128)S(1)}, u32[]{:S(2)}, u32[]{:S(2)}) %collective-permute-start.1) | collective-permute-done | bytes 131104 | tf_op jit(solution)/shard_map/ppermute | solution.py:45
  106.4 10.8 %collective-permute-done.2 = f32[16,16,128]{2,1,0:T(8,128)S(1)} collective-permute-done((f32[16,16,128]{2,1,0:T(8,128)S(1)}, f32[16,16,128]{2,1,0:T(8,128)S(1)}, u32[]{:S(2)}, u32[]{:S(2)}) %collective-permute-start.2) | collective-permute-done | bytes 131104 | tf_op jit(solution)/shard_map/ppermute | solution.py:45
  117.2 10.6 %collective-permute-done.3 = f32[16,16,128]{2,1,0:T(8,128)S(1)} collective-permute-done((f32[16,16,128]{2,1,0:T(8,128)S(1)}, f32[16,16,128]{2,1,0:T(8,128)S(1)}, u32[]{:S(2)}, u32[]{:S(2)}) %collective-permute-start.3) | collective-permute-done | bytes 131104 | tf_op jit(solution)/shard_map/ppermute | solution.py:45
  127.8 10.6 %collective-permute-done.4 = f32[16,16,128]{2,1,0:T(8,128)S(1)} collective-permute-done((f32[16,16,128]{2,1,0:T(8,128)S(1)}, f32[16,16,128]{2,1,0:T(8,128)S(1)}, u32[]{:S(2)}, u32[]{:S(2)}) %collective-permute-start.4) | collective-permute-done | bytes 131104 | tf_op jit(solution)/shard_map/ppermute | solution.py:45
  138.4 7.8 %collective-permute-done.5 = f32[16,16,128]{2,1,0:T(8,128)} collective-permute-done((f32[16,16,128]{2,1,0:T(8,128)S(1)}, f32[16,16,128]{2,1,0:T(8,128)}, u32[]{:S(2)}, u32[]{:S(2)}) %collective-permute-start.5) | collective-permute-done | bytes 131104 | tf_op jit(solution)/shard_map/ppermute | solution.py:45
  147.0 10.2 %collective-permute-done.6 = f32[16,16,128]{2,1,0:T(8,128)} collective-permute-done((f32[16,16,128]{2,1,0:T(8,128)}, f32[16,16,128]{2,1,0:T(8,128)}, u32[]{:S(2)}, u32[]{:S(2)}) %collective-permute-start.6) | collective-permute-done | bytes 131104 | tf_op jit(solution)/shard_map/ppermute | solution.py:45
  157.1 1.6 constant_dynamic-update-slice_fusion.15
  158.7 1.6 constant_dynamic-update-slice_fusion.14
  160.3 1.6 constant_dynamic-update-slice_fusion.13
  161.9 1.6 constant_dynamic-update-slice_fusion.12
  163.4 1.6 constant_dynamic-update-slice_fusion.11
  167.1 1.6 constant_dynamic-update-slice_fusion.7
  168.7 1.6 constant_dynamic-update-slice_fusion.6
  170.3 0.7 constant_dynamic-update-slice_fusion.5
  173.1 0.7 constant_dynamic-update-slice_fusion.1
  174.4 43.9 %all-gather.4.cloned.1.call-done = f32[128,128,128]{2,1,0:T(8,128)} async-done(((f32[16,128,128]{2,1,0:T(8,128)}), f32[128,128,128]{2,1,0:T(8,128)}) %all-gather.4.cloned.1.call-update) | async-done | bytes 8388624 | tf_op jit(solution)/shard_map/all_gather | solution.py:13
  218.4 11.3 %while.29 = (s32[]{:T(128)}, f32[16,128,128]{2,1,0:T(8,128)S(1)}, s32[]{:T(128)}, f32[8,16,128,128]{3,2,1,0:T(8,128)}, s32[]{:T(128)}, /*index=5*/s32[]{:T(128)}) while((s32[]{:T(128)}, f32[16,128,128]{2,1,0:T(8,128)S(1)}, s32[]{:T(128)}, f32[8,16,128,128]{3,2,1,0:T(8,128)}, s32[]{:T(128)}, /*index=5*/s32[]{:T(128)}) %tuple.70), condition=%wide.region_4.5_spmd.clone, body=%wide.region_3.4_spmd.clone.sunk | while | flops 786436 | bytes 3145829 | solution.py:20
  218.4 1.6 add_select_fusion.5
  220.0 1.6 add_select_fusion.5
  221.6 1.6 add_select_fusion.5
  223.2 1.6 add_select_fusion.5
  224.8 1.6 add_select_fusion.5
  226.4 1.6 add_select_fusion.5
  228.0 1.6 add_select_fusion.5
  229.7 1.8 multiply_reduce_fusion
  231.8 1.0 copy.16
  (45 shorter events, 6.9 us)
Async XLA Ops:
  6.5 139.7 %copy-start = (bf16[128,2048]{1,0:T(8,128)(2,1)S(1)}, bf16[128,2048]{1,0:T(8,128)(2,1)}, u32[]{:S(2)}) copy-start(bf16[128,2048]{1,0:T(8,128)(2,1)} %param.8) | copy-start | bytes 1572868
  6.5 71.7 %reduce-scatter.2.cloned.1.call-start = ((), (), s32[]{:S(2)}) async-start(), calls=%async_computation.1 | async-start | bytes 1179648 | tf_op jit(solution)/shard_map/reduce_scatter | solution.py:39
  10.2 136.0 %copy-start.1 = (bf16[128,2048]{1,0:T(8,128)(2,1)S(1)}, bf16[128,2048]{1,0:T(8,128)(2,1)}, u32[]{:S(2)}) copy-start(bf16[128,2048]{1,0:T(8,128)(2,1)} %param.10) | copy-start | bytes 1572868
  10.3 208.1 %all-gather.4.cloned.1.call-start = ((), (), s32[]{:S(2)}) async-start(), calls=%async_computation.2 | async-start | bytes 9437184 | tf_op jit(solution)/shard_map/all_gather | solution.py:13
  85.7 9.7 %collective-permute-start = (f32[16,16,128]{2,1,0:T(8,128)S(1)}, f32[16,16,128]{2,1,0:T(8,128)S(1)}, u32[]{:S(2)}, u32[]{:S(2)}) collective-permute-start(f32[16,16,128]{2,1,0:T(8,128)S(1)} %get-tuple-element.163), channel_id=1, source_target_pairs={{0,1},{1,2},{2,3},{3,4},{4,5},{5,6},{6,7},{7,0},{8,9},{9,10},{10,1... | collective-permute-start | bytes 393224 | tf_op jit(solution)/shard_map/ppermute | solution.py:45
  95.4 11.0 %collective-permute-start.1 = (f32[16,16,128]{2,1,0:T(8,128)S(1)}, f32[16,16,128]{2,1,0:T(8,128)S(1)}, u32[]{:S(2)}, u32[]{:S(2)}) collective-permute-start(f32[16,16,128]{2,1,0:T(8,128)S(1)} %collective-permute-done), channel_id=1, source_target_pairs={{0,1},{1,2},{2,3},{3,4},{4,5},{5,6},{6,7},{7,0},{8,9},{9,10},{10,1... | collective-permute-start | bytes 393224 | tf_op jit(solution)/shard_map/ppermute | solution.py:45
  106.4 10.8 %collective-permute-start.2 = (f32[16,16,128]{2,1,0:T(8,128)S(1)}, f32[16,16,128]{2,1,0:T(8,128)S(1)}, u32[]{:S(2)}, u32[]{:S(2)}) collective-permute-start(f32[16,16,128]{2,1,0:T(8,128)S(1)} %collective-permute-done.1), channel_id=1, source_target_pairs={{0,1},{1,2},{2,3},{3,4},{4,5},{5,6},{6,7},{7,0},{8,9},{9,10},{10,1... | collective-permute-start | bytes 393224 | tf_op jit(solution)/shard_map/ppermute | solution.py:45
  117.2 29.7 %copy-start.2 = (f32[16,16,128]{2,1,0:T(8,128)}, f32[16,16,128]{2,1,0:T(8,128)S(1)}, u32[]{:S(2)}) copy-start(f32[16,16,128]{2,1,0:T(8,128)S(1)} %collective-permute-done.2) | copy-start | bytes 393220
  117.2 10.6 %collective-permute-start.3 = (f32[16,16,128]{2,1,0:T(8,128)S(1)}, f32[16,16,128]{2,1,0:T(8,128)S(1)}, u32[]{:S(2)}, u32[]{:S(2)}) collective-permute-start(f32[16,16,128]{2,1,0:T(8,128)S(1)} %collective-permute-done.2), channel_id=1, source_target_pairs={{0,1},{1,2},{2,3},{3,4},{4,5},{5,6},{6,7},{7,0},{8,9},{9,10},{10,1... | collective-permute-start | bytes 393224 | tf_op jit(solution)/shard_map/ppermute | solution.py:45
  127.8 19.1 %copy-start.4 = (f32[16,16,128]{2,1,0:T(8,128)}, f32[16,16,128]{2,1,0:T(8,128)S(1)}, u32[]{:S(2)}) copy-start(f32[16,16,128]{2,1,0:T(8,128)S(1)} %collective-permute-done.3) | copy-start | bytes 393220
  127.8 10.6 %collective-permute-start.4 = (f32[16,16,128]{2,1,0:T(8,128)S(1)}, f32[16,16,128]{2,1,0:T(8,128)S(1)}, u32[]{:S(2)}, u32[]{:S(2)}) collective-permute-start(f32[16,16,128]{2,1,0:T(8,128)S(1)} %collective-permute-done.3), channel_id=1, source_target_pairs={{0,1},{1,2},{2,3},{3,4},{4,5},{5,6},{6,7},{7,0},{8,9},{9,10},{10,1... | collective-permute-start | bytes 393224 | tf_op jit(solution)/shard_map/ppermute | solution.py:45
  138.4 8.5 %copy-start.6 = (f32[16,16,128]{2,1,0:T(8,128)}, f32[16,16,128]{2,1,0:T(8,128)S(1)}, u32[]{:S(2)}) copy-start(f32[16,16,128]{2,1,0:T(8,128)S(1)} %collective-permute-done.4) | copy-start | bytes 393220
  138.4 7.8 %collective-permute-start.5 = (f32[16,16,128]{2,1,0:T(8,128)S(1)}, f32[16,16,128]{2,1,0:T(8,128)}, u32[]{:S(2)}, u32[]{:S(2)}) collective-permute-start(f32[16,16,128]{2,1,0:T(8,128)S(1)} %collective-permute-done.4), channel_id=1, source_target_pairs={{0,1},{1,2},{2,3},{3,4},{4,5},{5,6},{6,7},{7,0},{8,9},{9,10},{10,1... | collective-permute-start | bytes 393224 | tf_op jit(solution)/shard_map/ppermute | solution.py:45
  146.2 10.9 %collective-permute-start.6 = (f32[16,16,128]{2,1,0:T(8,128)}, f32[16,16,128]{2,1,0:T(8,128)}, u32[]{:S(2)}, u32[]{:S(2)}) collective-permute-start(f32[16,16,128]{2,1,0:T(8,128)} %collective-permute-done.5), channel_id=1, source_target_pairs={{0,1},{1,2},{2,3},{3,4},{4,5},{5,6},{6,7},{7,0},{8,9},{9,10},{10,1... | collective-permute-start | bytes 393224 | tf_op jit(solution)/shard_map/ppermute | solution.py:45
  146.9 23.4 %copy-start.7 = (f32[16,16,128]{2,1,0:T(8,128)S(1)}, f32[16,16,128]{2,1,0:T(8,128)}, u32[]{:S(2)}) copy-start(f32[16,16,128]{2,1,0:T(8,128)} %copy-done.6) | copy-start | bytes 393220
  146.9 24.1 %copy-start.5 = (f32[16,16,128]{2,1,0:T(8,128)S(1)}, f32[16,16,128]{2,1,0:T(8,128)}, u32[]{:S(2)}) copy-start(f32[16,16,128]{2,1,0:T(8,128)} %copy-done.4) | copy-start | bytes 393220
  147.0 24.7 %copy-start.3 = (f32[16,16,128]{2,1,0:T(8,128)S(1)}, f32[16,16,128]{2,1,0:T(8,128)}, u32[]{:S(2)}) copy-start(f32[16,16,128]{2,1,0:T(8,128)} %copy-done.2) | copy-start | bytes 393220
  229.6 1.8 copy-start.8
Sparse Core Ops, SparseCore 0:
  10.7 67.4 reduce-scatter.1
  80.3 137.9 all-gather.3
